TPU v7x, 32 devices: a whole 2x2x4 slice. The times are simulated.
32 devices in a mesh: grp: 2 (over y), ctx: 4 (over z), sub: 4 (over x, core).
Axes of the slice: x: 2, y: 2, z: 4, core: 2. Of those that a mesh axis runs over, the one named last changes fastest.
Arguments:
- query_rows: bfloat16 [8192, 1024], P(('grp', 'ctx', 'sub')), parts along dimension 0, may hold values from -6 to 6
- key_rows: bfloat16 [8192, 1024], P(('grp', 'ctx', 'sub')), parts along dimension 0, may hold values from -6 to 6
- value_rows: bfloat16 [8192, 1024], P(('grp', 'ctx', 'sub')), parts along dimension 0, may hold values from -6 to 6
- out_grad: bfloat16 [8192, 1024], P(('grp', 'ctx', 'sub')), parts along dimension 0, may hold values from -6 to 6
- reg_query: bfloat16 [6144, 1024], P(('grp', 'ctx', 'sub')), parts along dimension 0, may hold values from -6 to 6
- reg_out_grad: bfloat16 [6144, 1024], P(('grp', 'ctx', 'sub')), parts along dimension 0, may hold values from -6 to 6
- reg_offset: int32 [6144], P(('grp', 'ctx', 'sub')), parts along dimension 0, may hold values from 0 to 255
Outputs:
- grad_query: bfloat16 [8192, 1024], P(('grp', 'ctx', 'sub')), parts along dimension 0
- grad_key: bfloat16 [8192, 1024], P(('grp', 'ctx', 'sub')), parts along dimension 0
- grad_value: bfloat16 [8192, 1024], P(('grp', 'ctx', 'sub')), parts along dimension 0
- grad_reg_query: bfloat16 [6144, 1024], P(('grp', 'ctx', 'sub')), parts along dimension 0
There are 2 independent parts, one for each index of `grp`. A program takes and returns all parts, laid end to end along the dimension named above; each array names one. Nothing has to cross between parts.
All inputs are finite; a program needn't handle non-finite values.
Results may differ from a plain program's by a relative error of at most 0.0049.
Values sent between devices are 32-bit elements; how exact they have to be, the bound alone decides.
A program may use at most 128 MiB of HBM per device.

v0:
```python
import math

import jax
import jax.numpy as jnp
from jax import lax
from jax.sharding import PartitionSpec as P

HEADS = 8
HEAD = 128


def carried_in(value, axis, join, neutral, backward):
    count, mine = (lax.axis_size(axis), lax.axis_index(axis))
    pieces = lax.all_gather(value, axis)
    if backward:
        pieces = pieces[::-1]
        mine = count - 1 - mine
    running = jnp.full_like(value, 0) + jnp.asarray(neutral, value.dtype)

    def hop(position, running):
        longer = join(running, pieces[position])
        return jnp.where(position < mine, longer, running)

    return lax.fori_loop(0, count - 1, hop, running)


def add_one(earlier, later):
    return earlier + later


def local(query_rows, key_rows, value_rows, out_grad, reg_query, reg_out_grad, reg_offset):
    row_count = query_rows.shape[0]
    reg_count = reg_query.shape[0]
    total_rows = row_count * lax.axis_size("ctx") * lax.axis_size("sub")
    factor = 1.0 / math.sqrt(HEAD * total_rows)
    query_heads = query_rows.reshape(row_count, HEADS, HEAD)
    key_heads = key_rows.reshape(row_count, HEADS, HEAD)
    value_heads = value_rows.reshape(row_count, HEADS, HEAD)
    grad_heads = out_grad.reshape(row_count, HEADS, HEAD)
    regq_heads = reg_query.reshape(reg_count, HEADS, HEAD)
    regg_heads = reg_out_grad.reshape(reg_count, HEADS, HEAD)
    kv_local = jnp.einsum(
        "shd,she->hde", key_heads, value_heads, preferred_element_type=jnp.float32
    )
    grad_local = jnp.einsum(
        "thd,the->hde", query_heads, grad_heads, preferred_element_type=jnp.float32
    ) + jnp.einsum("jhd,jhe->hde", regq_heads, regg_heads, preferred_element_type=jnp.float32)
    every_kv, every_grad = (
        lax.all_gather(kv_local[None], "sub", axis=0, tiled=True),
        lax.all_gather(grad_local[None], "sub", axis=0, tiled=True),
    )
    sub_count = lax.axis_size("sub")
    position = lax.axis_index("sub")
    slots = jnp.arange(sub_count, dtype=jnp.int32)
    earlier_mask = (slots < position)[:, None, None, None]
    later_mask = (slots > position)[:, None, None, None]
    zero_value = jnp.float32(0.0)
    inner_kv = jnp.sum(jnp.where(earlier_mask, every_kv, zero_value), axis=0)
    inner_grad = jnp.sum(jnp.where(later_mask, every_grad, zero_value), axis=0)
    share_rows = kv_local.shape[1] // sub_count
    start_row = position * share_rows
    share_kv = lax.dynamic_slice_in_dim(jnp.sum(every_kv, axis=0), start_row, share_rows, 1)
    share_grad = lax.dynamic_slice_in_dim(jnp.sum(every_grad, axis=0), start_row, share_rows, 1)
    share_zero = jnp.zeros_like(share_kv)
    outer_kv = carried_in(share_kv, "ctx", add_one, share_zero, False)
    outer_grad = carried_in(share_grad, "ctx", add_one, share_zero, True)
    full_kv, full_grad = (
        lax.all_gather(outer_kv, "sub", axis=1, tiled=True),
        lax.all_gather(outer_grad, "sub", axis=1, tiled=True),
    )
    before = (full_kv + inner_kv).astype(jnp.bfloat16)
    after = (full_grad + inner_grad).astype(jnp.bfloat16)
    row_index = jnp.arange(row_count, dtype=jnp.int32)
    causal = row_index[:, None] >= row_index[None, :]
    reg_mask = reg_offset[:, None] >= row_index[None, :]
    zero = jnp.float32(0.0)
    out_scores = jnp.where(
        causal,
        jnp.einsum("the,she->hts", grad_heads, value_heads, preferred_element_type=jnp.float32),
        zero,
    ).astype(jnp.bfloat16)
    qk_scores = jnp.where(
        causal,
        jnp.einsum("thd,shd->hts", query_heads, key_heads, preferred_element_type=jnp.float32),
        zero,
    ).astype(jnp.bfloat16)
    reg_out_scores = jnp.where(
        reg_mask,
        jnp.einsum("jhe,she->hjs", regg_heads, value_heads, preferred_element_type=jnp.float32),
        zero,
    ).astype(jnp.bfloat16)
    reg_qk_scores = jnp.where(
        reg_mask,
        jnp.einsum("jhd,shd->hjs", regq_heads, key_heads, preferred_element_type=jnp.float32),
        zero,
    ).astype(jnp.bfloat16)
    grad_q = jnp.einsum(
        "hts,shd->thd", out_scores, key_heads, preferred_element_type=jnp.float32
    ) + jnp.einsum("the,hde->thd", grad_heads, before, preferred_element_type=jnp.float32)
    grad_rq = jnp.einsum(
        "hjs,shd->jhd", reg_out_scores, key_heads, preferred_element_type=jnp.float32
    ) + jnp.einsum("jhe,hde->jhd", regg_heads, before, preferred_element_type=jnp.float32)
    grad_k = (
        jnp.einsum("hts,thd->shd", out_scores, query_heads, preferred_element_type=jnp.float32)
        + jnp.einsum("hjs,jhd->shd", reg_out_scores, regq_heads, preferred_element_type=jnp.float32)
        + jnp.einsum("she,hde->shd", value_heads, after, preferred_element_type=jnp.float32)
    )
    grad_v = (
        jnp.einsum("hts,the->she", qk_scores, grad_heads, preferred_element_type=jnp.float32)
        + jnp.einsum("hjs,jhe->she", reg_qk_scores, regg_heads, preferred_element_type=jnp.float32)
        + jnp.einsum("shd,hde->she", key_heads, after, preferred_element_type=jnp.float32)
    )
    width = HEADS * HEAD
    return (
        (grad_q * factor).astype(jnp.bfloat16).reshape(row_count, width),
        (grad_k * factor).astype(jnp.bfloat16).reshape(row_count, width),
        (grad_v * factor).astype(jnp.bfloat16).reshape(row_count, width),
        (grad_rq * factor).astype(jnp.bfloat16).reshape(reg_count, width),
    )


def solution(mesh):
    placed = (
        P(("grp", "ctx", "sub"), None),
        P(("grp", "ctx", "sub"), None),
        P(("grp", "ctx", "sub"), None),
        P(("grp", "ctx", "sub"), None),
        P(("grp", "ctx", "sub"), None),
        P(("grp", "ctx", "sub"), None),
        P(("grp", "ctx", "sub")),
    )
    return jax.shard_map(
        local,
        mesh=mesh,
        in_specs=placed,
        out_specs=(
            P(("grp", "ctx", "sub"), None),
            P(("grp", "ctx", "sub"), None),
            P(("grp", "ctx", "sub"), None),
            P(("grp", "ctx", "sub"), None),
        ),
        check_vma=False,
    )
```

profile of v0, /device:TPU:0, one launch (start us, length us, event | category | flops | bytes accessed | tf_op | source)
XLA Modules:
  0.0 112.0 jit_solution(8442415530743410559)
XLA Ops:
  7.2 1.3 %copy.90 = bf16[256,1024]{0,1:T(8,128)(2,1)S(1)} copy(bf16[256,1024]{1,0:T(8,128)(2,1)} %param.14) | data formatting | bytes 1048576 | tf_op jit(solution)/shard_map/reshape | solution.py:39
  8.6 1.5 %fusion.45 = f32[8,128,128]{2,1,0:T(8,128)S(1)} fusion(bf16[192,1024]{1,0:T(8,128)(2,1)} %param.15, bf16[192,1024]{1,0:T(8,128)(2,1)} %param.16), kind=kOutput, calls=%fused_computation.59 | convolution fusion | flops 50331648 | bytes 1310720 | tf_op jit(solution)/shard_map/jhd,jhe->hde/dot_general | solution.py:47
  10.1 1.1 %convolution_add_fusion.1 = f32[8,128,128]{2,1,0:T(8,128)} fusion(f32[8,128,128]{2,1,0:T(8,128)S(1)} %fusion.45, bf16[256,8,128]{0,2,1:T(8,128)(2,1)S(1)} %bitcast.193, bf16[256,1024]{1,0:T(8,128)(2,1)S(1)} %copy-done.1), kind=kOutput, calls=%fused_computation.32 | convolution fusion | flops 67239936 | bytes 2097152 | tf_op jit(solution)/shard_map/thd,the->hde/dot_general | solution.py:45
  11.4 1.1 %fusion.26 = f32[8,128,128]{2,1,0:T(8,128)} fusion(bf16[256,1024]{1,0:T(8,128)(2,1)S(1)} %copy-done, bf16[256,1024]{1,0:T(8,128)(2,1)S(1)} %copy-done.9), kind=kOutput, calls=%fused_computation.41 | convolution fusion | flops 67108864 | bytes 1572864 | tf_op jit(solution)/shard_map/shd,she->hde/dot_general | solution.py:42
  12.7 1.4 %select_convert_fusion.3 = bf16[8,192,256]{2,1,0:T(8,128)(2,1)S(1)} fusion(pred[192,256]{1,0:T(8,128)(4,1)S(1)} %iota_compare_fusion.1, bf16[256,1024]{1,0:T(8,128)(2,1)S(1)} %copy-done.9, bf16[192,1024]{1,0:T(8,128)(2,1)} %param.16), kind=kOutput, calls=%fused_computation.7 | convolution fusion | flops 101449728 | bytes 1753088 | tf_op jit(solution)/shard_map/jhe,she->hjs/dot_general | solution.py:89
  14.1 0.9 copy-done.5
  15.0 1.3 %convolution_bitcast_fusion.4 = f32[192,8,128]{2,0,1:T(8,128)} fusion(bf16[8,192,256]{2,1,0:T(8,128)(2,1)S(1)} %select_convert_fusion.3, bf16[256,1024]{1,0:T(8,128)(2,1)S(1)} %copy-done), kind=kOutput, calls=%fused_computation.27 | convolution fusion | flops 100663296 | bytes 2097152 | tf_op jit(solution)/shard_map/hjs,shd->jhd/dot_general | solution.py:100
  16.8 0.6 copy-done.6
  17.5 1.3 %fusion.47 = f32[8,256,128]{1,2,0:T(8,128)} fusion(bf16[8,192,256]{2,1,0:T(8,128)(2,1)S(1)} %copy-done.6, bf16[192,1024]{1,0:T(8,128)(2,1)S(1)} %copy-done.15), kind=kOutput, calls=%fused_computation.61 | convolution fusion | flops 100663296 | bytes 2228224 | tf_op jit(solution)/shard_map/hjs,jhd->shd/dot_general | solution.py:105
  18.8 2.5 %fusion.13 = f32[8,256,128]{1,2,0:T(8,128)} fusion(pred[192,256]{1,0:T(8,128)(4,1)S(1)} %iota_compare_fusion.1, bf16[256,1024]{1,0:T(8,128)(2,1)S(1)} %copy-done, bf16[192,1024]{1,0:T(8,128)(2,1)} %param.15, bf16[192,1024]{1,0:T(8,128)(2,1)S(1)} %copy-done.13), kind=kOutput, calls=%fused_computation.26 | convolution fusion | flops 202113024 | bytes 2408448 | tf_op jit(solution)/shard_map/hjs,jhe->she/dot_general | solution.py:110
  21.3 1.5 %convolution_bitcast_fusion.3 = f32[256,8,128]{0,2,1:T(8,128)} fusion(bf16[8,256,256]{2,1,0:T(8,128)(2,1)S(1)} %select_convert_fusion.1, bf16[256,1024]{1,0:T(8,128)(2,1)S(1)} %copy-done), kind=kOutput, calls=%fused_computation.22 | convolution fusion | flops 134217728 | bytes 2621440 | tf_op jit(solution)/shard_map/hts,shd->thd/dot_general | solution.py:97
  22.8 1.8 %fusion.2 = f32[256,8,128]{0,2,1:T(8,128)S(1)} fusion(f32[8,256,128]{1,2,0:T(8,128)} %fusion.13, bf16[256,8,128]{0,2,1:T(8,128)(2,1)S(1)} %bitcast.195, pred[256,256]{1,0:T(8,128)(4,1)S(1)} %iota_compare_fusion, bf16[256,1024]{1,0:T(8,128)(2,1)S(1)} %copy-done.1, bf16[256,1024]{1,0:T(8,128)(2,1)S(1)} %copy-done), kind=kOutput, calls=%fused_computation.10 | convolution fusion | flops 269746176 | bytes 3735552 | tf_op jit(solution)/shard_map/hts,the->she/dot_general | solution.py:109
  24.6 12.1 %all-gather.9.cloned.1.call-done = f32[32,128,128]{2,1,0:T(8,128)} async-done(((f32[8,128,128]{2,1,0:T(8,128)}), f32[32,128,128]{2,1,0:T(8,128)}) %all-gather.9.cloned.1.call-update) | async-done | bytes 2097168 | tf_op jit(solution)/shard_map/all_gather | solution.py:50
  36.7 2.8 %select_reduce_fusion = (f32[8,128,128]{2,1,0:T(8,128)}, f32[8,128,128]{2,1,0:T(8,128)S(1)}) fusion(f32[4,8,128,128]{3,2,1,0:T(8,128)} %bitcast.200, pred[4]{0:T(512)(128)(4,1)S(1)} %iota_compare_fusion.2), kind=kLoop, calls=%fused_computation.3 | loop fusion | flops 1310720 | bytes 3145732 | tf_op jit(solution)/shard_map/reduce_sum | solution.py:59
  39.6 16.4 %all-gather.3 = f32[32,32,128]{2,1,0:T(8,128)} all-gather(f32[8,32,128]{2,1,0:T(8,128)S(1)} %constant_dynamic-slice_fusion), channel_id=5, replica_groups=mesh['grp'=2,'ctx'=4,'sub'=4] {'ctx'}, dimensions={0}, use_global_device_ids=true | all-gather | bytes 655360 | tf_op jit(solution)/shard_map/all_gather | solution.py:14
  56.0 1.1 rev.3
  57.2 7.0 %all_gather.31 = f32[8,128,128]{2,1,0:T(8,128)} all-gather(f32[8,32,128]{2,1,0:T(8,128)S(1)} %get-tuple-element.163), channel_id=1, replica_groups=mesh['grp'=2,'ctx'=4,'sub'=4] {'sub'}, dimensions={1}, use_global_device_ids=true | all-gather | bytes 655360 | tf_op jit(solution)/shard_map/all_gather | solution.py:69
  64.2 2.8 %select_reduce_fusion.1 = (f32[8,128,128]{2,1,0:T(8,128)}, f32[8,128,128]{2,1,0:T(8,128)S(1)}) fusion(f32[4,8,128,128]{3,2,1,0:T(8,128)} %bitcast.199, pred[4]{0:T(512)(128)(4,1)S(1)} %iota_compare_fusion.3), kind=kLoop, calls=%fused_computation.4 | loop fusion | flops 1310720 | bytes 3145732 | tf_op jit(solution)/shard_map/reduce_sum | solution.py:58
  67.0 17.2 %all-gather.1 = f32[32,32,128]{2,1,0:T(8,128)} all-gather(f32[8,32,128]{2,1,0:T(8,128)S(1)} %constant_dynamic-slice_fusion.1), channel_id=3, replica_groups=mesh['grp'=2,'ctx'=4,'sub'=4] {'ctx'}, dimensions={0}, use_global_device_ids=true | all-gather | bytes 655360 | tf_op jit(solution)/shard_map/all_gather | solution.py:14
  84.2 3.0 %while.28 = (s32[]{:T(128)}, f32[8,32,128]{2,1,0:T(8,128)S(1)}, s32[]{:T(128)}, f32[4,8,32,128]{3,2,1,0:T(8,128)}, s32[]{:T(128)}, /*index=5*/s32[]{:T(128)}) while((s32[]{:T(128)}, f32[8,32,128]{2,1,0:T(8,128)S(1)}, s32[]{:T(128)}, f32[4,8,32,128]{3,2,1,0:T(8,128)}, s32[]{:T(128)}, /*index=5*/s32[]{:T(128)}) %tuple.78), condition=%wide.region_2.3_spmd.clone, body=%wide.region_1.2_spmd.clone.sunk | while | flops 98308 | bytes 393317 | solution.py:24
  84.2 1.0 add_select_fusion.4
  85.3 1.0 add_select_fusion.4
  86.3 1.0 add_select_fusion.4
  87.2 7.0 %all_gather.27 = f32[8,128,128]{2,1,0:T(8,128)S(1)} all-gather(f32[8,32,128]{2,1,0:T(8,128)S(1)} %get-tuple-element.162), channel_id=1, replica_groups=mesh['grp'=2,'ctx'=4,'sub'=4] {'sub'}, dimensions={1}, use_global_device_ids=true | all-gather | bytes 655360 | tf_op jit(solution)/shard_map/all_gather | solution.py:68
  94.3 1.2 %add_convert_fusion.1 = bf16[8,128,128]{2,1,0:T(8,128)(2,1)S(1)} fusion(f32[8,128,128]{2,1,0:T(8,128)S(1)} %all_gather.27, f32[8,128,128]{2,1,0:T(8,128)} %get-tuple-element.208), kind=kLoop, calls=%fused_computation.53 | loop fusion | flops 262144 | bytes 1310720 | tf_op jit(solution)/shard_map/convert_element_type | solution.py:71
  96.2 0.9 copy.182
  97.1 1.3 %convolution_bitcast_fusion.1 = f32[256,8,128]{0,2,1:T(8,128)} fusion(bf16[8,128,128]{2,1,0:T(8,128)(2,1)S(1)} %add_convert_fusion, bf16[256,1024]{1,0:T(8,128)(2,1)S(1)} %copy-done.10), kind=kOutput, calls=%fused_computation.18 | convolution fusion | flops 67108864 | bytes 1835008 | tf_op jit(solution)/shard_map/she,hde->shd/dot_general | solution.py:106
  98.8 1.0 copy.88
  99.8 1.5 %fusion.10 = bf16[256,8,128]{0,2,1:T(8,128)(2,1)S(1)} fusion(f32[256,8,128]{0,2,1:T(8,128)} %convolution_bitcast_fusion.3, bf16[8,128,128]{2,1,0:T(8,128)(2,1)S(1)} %copy-done.8, bf16[256,8,128]{0,2,1:T(8,128)(2,1)S(1)} %bitcast.196), kind=kOutput, calls=%fused_computation.23 | convolution fusion | flops 67895296 | bytes 2359296 | tf_op jit(solution)/shard_map/the,hde->thd/dot_general | solution.py:99
  101.3 1.0 copy.86
  102.3 1.9 %fusion.12 = bf16[256,8,128]{0,2,1:T(8,128)(2,1)S(1)} fusion(f32[256,8,128]{0,2,1:T(8,128)S(1)} %copy-done.2, f32[8,256,128]{1,2,0:T(8,128)} %fusion.47, bf16[8,256,256]{2,1,0:T(8,128)(2,1)} %copy-done.3, bf16[256,1024]{1,0:T(8,128)(2,1)S(1)} %copy-done.1), kind=kOutput, calls=%fused_computation.25 | convolution fusion | flops 135266304 | bytes 4194304 | tf_op jit(solution)/shard_map/hts,thd->shd/dot_general | solution.py:104
  104.2 1.0 copy.87
  (53 shorter events, 2.3 us)
Async XLA Ops:
  7.2 4.2 %copy-start = (bf16[256,1024]{1,0:T(8,128)(2,1)S(1)}, bf16[256,1024]{1,0:T(8,128)(2,1)}, u32[]{:S(2)}) copy-start(bf16[256,1024]{1,0:T(8,128)(2,1)} %param.12) | copy-start | bytes 1572868
  7.2 2.9 %copy-start.1 = (bf16[256,1024]{1,0:T(8,128)(2,1)S(1)}, bf16[256,1024]{1,0:T(8,128)(2,1)}, u32[]{:S(2)}) copy-start(bf16[256,1024]{1,0:T(8,128)(2,1)} %param.11) | copy-start | bytes 1572868
  7.2 29.5 %all-gather.9.cloned.1.call-start = ((), (), s32[]{:S(2)}) async-start(), calls=%async_computation.1 | async-start | bytes 2621440 | tf_op jit(solution)/shard_map/all_gather | solution.py:50
  8.6 2.8 %copy-start.9 = (bf16[256,1024]{1,0:T(8,128)(2,1)S(1)}, bf16[256,1024]{1,0:T(8,128)(2,1)}, u32[]{:S(2)}) copy-start(bf16[256,1024]{1,0:T(8,128)(2,1)} %param.13) | copy-start | bytes 1572868
  10.1 2.5 %copy-start.16 = (s32[192]{0:T(256)S(1)}, s32[192]{0:T(256)}, u32[]{:S(2)}) copy-start(s32[192]{0:T(256)} %param.17) | copy-start | bytes 2308
  11.3 52.9 %all-gather.7.cloned.1.call-start = ((), (), s32[]{:S(2)}) async-start(), calls=%async_computation | async-start | bytes 2621440 | tf_op jit(solution)/shard_map/all_gather | solution.py:49
  14.1 0.9 copy-start.5
  15.0 1.8 %copy-start.15 = (bf16[192,1024]{1,0:T(8,128)(2,1)S(1)}, bf16[192,1024]{1,0:T(8,128)(2,1)}, u32[]{:S(2)}) copy-start(bf16[192,1024]{1,0:T(8,128)(2,1)} %param.15) | copy-start | bytes 1179652
  16.3 1.1 %copy-start.6 = (bf16[8,192,256]{2,1,0:T(8,128)(2,1)S(1)}, bf16[8,192,256]{2,1,0:T(8,128)(2,1)}, u32[]{:S(2)}) copy-start(bf16[8,192,256]{2,1,0:T(8,128)(2,1)} %copy-done.5) | copy-start | bytes 2359300
  17.5 3.9 %copy-start.3 = (bf16[8,256,256]{2,1,0:T(8,128)(2,1)}, bf16[8,256,256]{2,1,0:T(8,128)(2,1)S(1)}, u32[]{:S(2)}) copy-start(bf16[8,256,256]{2,1,0:T(8,128)(2,1)S(1)} %select_convert_fusion.1) | copy-start | bytes 3145732
  17.5 1.3 %copy-start.13 = (bf16[192,1024]{1,0:T(8,128)(2,1)S(1)}, bf16[192,1024]{1,0:T(8,128)(2,1)}, u32[]{:S(2)}) copy-start(bf16[192,1024]{1,0:T(8,128)(2,1)} %param.16) | copy-start | bytes 1179652
  84.2 11.2 %copy-start.4 = (f32[192,8,128]{2,0,1:T(8,128)S(1)}, f32[192,8,128]{2,0,1:T(8,128)}, u32[]{:S(2)}) copy-start(f32[192,8,128]{2,0,1:T(8,128)} %convolution_bitcast_fusion.4) | copy-start | bytes 2359300
  87.2 8.2 %copy-start.14 = (bf16[192,1024]{1,0:T(8,128)(2,1)S(1)}, bf16[192,1024]{1,0:T(8,128)(2,1)}, u32[]{:S(2)}) copy-start(bf16[192,1024]{1,0:T(8,128)(2,1)} %param.16) | copy-start | bytes 1179652
  94.3 2.8 %copy-start.11 = (f32[8,128,128]{2,1,0:T(8,128)S(1)}, f32[8,128,128]{2,1,0:T(8,128)}, u32[]{:S(2)}) copy-start(f32[8,128,128]{2,1,0:T(8,128)} %all_gather.31) | copy-start | bytes 1572868
  94.3 2.8 %copy-start.12 = (f32[8,128,128]{2,1,0:T(8,128)S(1)}, f32[8,128,128]{2,1,0:T(8,128)}, u32[]{:S(2)}) copy-start(f32[8,128,128]{2,1,0:T(8,128)} %get-tuple-element.206) | copy-start | bytes 1572868
  95.5 0.7 copy-start.7
  95.5 1.6 %copy-start.10 = (bf16[256,1024]{1,0:T(8,128)(2,1)S(1)}, bf16[256,1024]{1,0:T(8,128)(2,1)}, u32[]{:S(2)}) copy-start(bf16[256,1024]{1,0:T(8,128)(2,1)} %param.13) | copy-start | bytes 1572868
  98.4 1.4 %copy-start.8 = (bf16[8,128,128]{2,1,0:T(8,128)(2,1)S(1)}, bf16[8,128,128]{2,1,0:T(8,128)(2,1)}, u32[]{:S(2)}) copy-start(bf16[8,128,128]{2,1,0:T(8,128)(2,1)} %copy-done.7) | copy-start | bytes 786436
  98.8 3.5 %copy-start.2 = (f32[256,8,128]{0,2,1:T(8,128)S(1)}, f32[256,8,128]{0,2,1:T(8,128)}, u32[]{:S(2)}) copy-start(f32[256,8,128]{0,2,1:T(8,128)} %convolution_bitcast_fusion.1) | copy-start | bytes 3145732
Sparse Core Ops, SparseCore 0:
  11.4 25.2 all-gather.8
  38.9 22.5 all-gather.6
where the time goes:
time: 113 us; the launch traced here: 112 us
  blocking collectives  47.6 us (42%)
  matrix products  19.5 us (17%)
  between operations  14.3 us (13%)
  waiting for transfers between devices  12.1 us (11%)
  other arithmetic  10.1 us (9%)
  local copies, waits for them, and re-layouts  8.25 us (7%)
    all_gather x2, blocking collectives, carried_in(): pieces = lax.all_gather(value, axis)  33.6 us
    all_gather x1, waiting for transfers between devices, local(): lax.all_gather(grad_local[None], 'sub', axis=0, tiled=True)  12.1 us
    all_gather x1, blocking collectives, local(): lax.all_gather(outer_kv, 'sub', axis=1, tiled=True)  7.01 us
    all_gather x1, blocking collectives, local(): lax.all_gather(outer_grad, 'sub', axis=1, tiled=True)  6.95 us
    unnamed x37, local copies, waits for them, and re-layouts  4.97 us
    select_n x6, other arithmetic, hop(): return jnp.where(position < mine, longer, running)  3.07 us
    reduce_sum x1, other arithmetic, local(): inner_kv = jnp.sum(jnp.where(earlier_mask, every_kv, zero_value), axis=0)  2.82 us
    reduce_sum x1, other arithmetic, local(): inner_grad = jnp.sum(jnp.where(later_mask, every_grad, zero_value), axis=0)  2.82 us
  transfers between devices with their start and end apart: 2, of which 1 were waited for; matrix products, arithmetic and copies ran while one was open for 14% of the time, Pallas kernels for 0%

commit v1 on v0

--- a/solution.py
+++ b/solution.py
@@ -1,12 +1,16 @@
+import functools
 import math
 
 import jax
 import jax.numpy as jnp
 from jax import lax
+from jax.experimental import pallas as pl
+from jax.experimental.pallas import tpu as pltpu
 from jax.sharding import PartitionSpec as P
 
 HEADS = 8
 HEAD = 128
+MESH = pl.DeviceIdType.MESH
 
 
 def carried_in(value, axis, join, neutral, backward):
@@ -119,6 +123,295 @@
     )
 
 
+def contract(lhs, rhs, lhs_dim, rhs_dim):
+    return lax.dot_general(
+        lhs, rhs, (((lhs_dim,), (rhs_dim,)), ((), ())), preferred_element_type=jnp.float32
+    )
+
+
+def kernel(
+    factor,
+    q_hbm, k_hbm, v_hbm, g_hbm, rq_hbm, rg_hbm, off_ref,
+    out_q, out_k, out_v, out_rq,
+    qa, ga, ka, va, mine, pair, cross_out, cross_in, chain_in, chain_out, other, full, full16,
+    acc_q, acc_k, acc_v,
+    load_sem, pair_send, pair_recv, cross_send, cross_recv, chain_send, chain_recv,
+    own_send, other_send, relay_send, full_recv,
+):
+    ctx_count, sub_count = lax.axis_size("ctx"), lax.axis_size("sub")
+    each = HEADS // sub_count
+    z, s = lax.axis_index("ctx"), lax.axis_index("sub")
+    a, c = s // 2, s % 2
+    partner = {"sub": 2 * a + 1 - c}
+    across = {"sub": 2 * (1 - a) + c}
+    rows, regs = ka.shape[0], rq_hbm.shape[0]
+
+    loads = [
+        pltpu.make_async_copy(k_hbm, ka, load_sem.at[0]),
+        pltpu.make_async_copy(v_hbm, va, load_sem.at[1]),
+        pltpu.make_async_copy(q_hbm, qa.at[pl.ds(0, rows)], load_sem.at[2]),
+        pltpu.make_async_copy(g_hbm, ga.at[pl.ds(0, rows)], load_sem.at[3]),
+        pltpu.make_async_copy(rq_hbm, qa.at[pl.ds(rows, regs)], load_sem.at[4]),
+        pltpu.make_async_copy(rg_hbm, ga.at[pl.ds(rows, regs)], load_sem.at[5]),
+    ]
+    for load in loads:
+        load.start()
+
+    barrier = pltpu.get_barrier_semaphore()
+    has_prev, has_next = z > 0, z < ctx_count - 1
+    for target in (partner, across):
+        pl.semaphore_signal(barrier, inc=1, device_id=target, device_id_type=MESH)
+
+    @pl.when(has_prev)
+    def _():
+        pl.semaphore_signal(barrier, inc=1, device_id={"ctx": z - 1}, device_id_type=MESH)
+
+    @pl.when(has_next)
+    def _():
+        pl.semaphore_signal(barrier, inc=1, device_id={"ctx": z + 1}, device_id_type=MESH)
+
+    def cols(h):
+        return pl.ds(pl.multiple_of(h * HEAD, HEAD), HEAD)
+
+    def remote(src, dst, send, recv, target):
+        return pltpu.make_async_remote_copy(
+            src_ref=src, dst_ref=dst, send_sem=send, recv_sem=recv,
+            device_id=target, device_id_type=MESH,
+        )
+
+    def pair_copy(k, h):
+        return remote(mine.at[k, h], pair.at[k, h], pair_send.at[k, h], pair_recv.at[k, h], partner)
+
+    def cross_copy(k, i):
+        return remote(
+            cross_out.at[k, i], cross_in.at[k, i], cross_send.at[k, i], cross_recv.at[k, i], across
+        )
+
+    def chain_copy(k, i, target):
+        return remote(
+            chain_out.at[k, i], chain_in.at[k, i], chain_send.at[k, i], chain_recv.at[k, i],
+            {"ctx": target},
+        )
+
+    def own_copy(k, i):
+        h = s * each + i
+        return remote(full.at[k, h], full.at[k, h], own_send.at[k, i], full_recv.at[k, h], partner)
+
+    def other_copy(k, i):
+        return remote(
+            other.at[k, i], full.at[k, s * each + i], other_send.at[k, i],
+            full_recv.at[k, s * each + i], across,
+        )
+
+    def relay_copy(k, i):
+        h = across["sub"] * each + i
+        return remote(full.at[k, h], full.at[k, h], relay_send.at[k, i], full_recv.at[k, h], partner)
+
+    first = jnp.where(2 * z >= ctx_count, 1, 0)
+    kinds = (first, 1 - first)
+
+    def state(h):
+        mine[0, h] = contract(ka[:, cols(h)], va[:, cols(h)], 0, 0)
+        mine[1, h] = contract(qa[:, cols(h)], ga[:, cols(h)], 0, 0)
+
+    for load in loads:
+        load.wait()
+    greeted = 2 + jnp.where(has_prev, 1, 0) + jnp.where(has_next, 1, 0)
+
+    for i in range(each):
+        state((2 * (1 - a) + 1 - c) * each + i)
+    pl.semaphore_wait(barrier, greeted)
+    for i in range(each):
+        for k in kinds:
+            pair_copy(k, (2 * (1 - a) + 1 - c) * each + i).start()
+    for i in range(each):
+        state(across["sub"] * each + i)
+    for i in range(each):
+        state((2 * a + 1 - c) * each + i)
+    for i in range(each):
+        for k in kinds:
+            pair_copy(k, (2 * a + 1 - c) * each + i).start()
+
+    for k in kinds:
+        for i in range(each):
+            h = across["sub"] * each + i
+            pair_copy(k, h).wait_recv()
+            cross_out[k, i] = mine[k, h] + pair[k, h]
+    for k in kinds:
+        for i in range(each):
+            cross_copy(k, i).start()
+    for i in range(each):
+        state(s * each + i)
+    for side in range(2):
+        for i in range(each):
+            pair_copy(c, (2 * side + c) * each + i).start()
+
+    place = lax.broadcasted_iota(jnp.int32, (rows, rows), 0)
+    time = lax.broadcasted_iota(jnp.int32, (rows, rows), 1)
+    reg_place = lax.broadcasted_iota(jnp.int32, (rows, regs), 0)
+
+    def masked(scores):
+        zero = jnp.float32(0.0)
+        regular = jnp.where(time >= place, scores[:, :rows], zero)
+        register = jnp.where(off_ref[...] >= reg_place, scores[:, rows:], zero)
+        return jnp.concatenate([regular, register], axis=1).astype(jnp.bfloat16)
+
+    def scores(h):
+        at = cols(h)
+        key, value, query, grad = ka[:, at], va[:, at], qa[:, at], ga[:, at]
+        out_scores = masked(contract(value, grad, 1, 1))
+        qk_scores = masked(contract(key, query, 1, 1))
+        acc_q[:, at] = contract(out_scores, key, 0, 0)
+        acc_k[:, at] = contract(out_scores, query, 1, 0)
+        acc_v[:, at] = contract(qk_scores, grad, 1, 0)
+
+    def some_scores(low, high):
+        lax.fori_loop(low, high, lambda h, _: (scores(h), 0)[1], 0)
+
+    def chain(k):
+        has_in = jnp.where(k == 0, has_prev, has_next)
+        has_out = jnp.where(k == 0, has_next, has_prev)
+        target = jnp.where(k == 0, z + 1, z - 1)
+        ahead = a == k
+        for i in range(each):
+            h = s * each + i
+            pair_copy(k, h).wait_recv()
+            cross_copy(k, i).wait_recv()
+
+            @pl.when(has_in)
+            def _():
+                chain_copy(k, i, target).wait_recv()
+
+            @pl.when(jnp.logical_not(has_in))
+            def _():
+                chain_in[k, i] = jnp.zeros((HEAD, HEAD), jnp.float32)
+
+            @pl.when(has_out)
+            def _():
+                chain_out[k, i] = (chain_in[k, i] + (mine[k, h] + pair[k, h])) + cross_in[k, i]
+                chain_copy(k, i, target).start()
+
+            carried = chain_in[k, i]
+            zero = jnp.float32(0.0)
+            own = mine[k, h] + pair[k, h]
+            other[k, i] = carried + jnp.where(ahead, own, zero)
+            other_copy(k, i).start()
+            full[k, h] = carried + jnp.where(ahead, zero, cross_in[k, i])
+            own_copy(k, i).start()
+
+    some_scores(0, 3)
+    chain(kinds[0])
+    some_scores(3, 6)
+    chain(kinds[1])
+    some_scores(6, HEADS)
+
+    for k in kinds:
+        for i in range(each):
+            other_copy_in = remote(
+                other.at[k, i], full.at[k, across["sub"] * each + i], other_send.at[k, i],
+                full_recv.at[k, across["sub"] * each + i], across,
+            )
+            other_copy_in.wait_recv()
+            relay_copy(k, i).start()
+
+    def full_wait(k, h):
+        remote(full.at[k, h], full.at[k, h], own_send.at[0, 0], full_recv.at[k, h], partner).wait_recv()
+
+    for side in range(2):
+        for i in range(each):
+            pair_copy(1 - c, (2 * side + 1 - c) * each + i).wait_recv()
+
+    def finish(h):
+        at = cols(h)
+        full16[1 - c, h] = (full[1 - c, h] + pair[1 - c, h]).astype(jnp.bfloat16)
+        full16[c, h] = full[c, h].astype(jnp.bfloat16)
+        before, after = full16[0, h], full16[1, h]
+        whole = (acc_q[:, at] + contract(ga[:, at], before, 1, 1)) * factor
+        out_q[:, at] = whole[:rows].astype(jnp.bfloat16)
+        out_rq[:, at] = whole[rows:].astype(jnp.bfloat16)
+        out_k[:, at] = ((acc_k[:, at] + contract(va[:, at], after, 1, 1)) * factor).astype(jnp.bfloat16)
+        out_v[:, at] = ((acc_v[:, at] + contract(ka[:, at], after, 1, 0)) * factor).astype(jnp.bfloat16)
+
+    for i in range(each):
+        finish(s * each + i)
+    for i in range(each):
+        finish(across["sub"] * each + i)
+    for i in range(each):
+        h = (2 * a + 1 - c) * each + i
+        full_wait(0, h)
+        full_wait(1, h)
+        finish(h)
+    for i in range(each):
+        h = (2 * (1 - a) + 1 - c) * each + i
+        full_wait(0, h)
+        full_wait(1, h)
+        finish(h)
+
+    for k in range(2):
+        for i in range(each):
+            for side in range(2):
+                pair_copy(k, (2 * side + 1 - c) * each + i).wait_send()
+            cross_copy(k, i).wait_send()
+            other_copy(k, i).wait_send()
+            own_copy(k, i).wait_send()
+            relay_copy(k, i).wait_send()
+
+            @pl.when((has_next, has_prev)[k])
+            def _():
+                chain_copy(k, i, (z + 1, z - 1)[k]).wait_send()
+    for side in range(2):
+        for i in range(each):
+            pair_copy(c, (2 * side + c) * each + i).wait_send()
+
+
+def fused(query_rows, key_rows, value_rows, out_grad, reg_query, reg_out_grad, reg_offset):
+    rows, width = query_rows.shape
+    regs = reg_query.shape[0]
+    sub_count = lax.axis_size("sub")
+    factor = 1.0 / math.sqrt(HEAD * rows * lax.axis_size("ctx") * sub_count)
+    each = HEADS // sub_count
+    all_states = pltpu.VMEM((2, HEADS, HEAD, HEAD), jnp.float32)
+    few_states = pltpu.VMEM((2, each, HEAD, HEAD), jnp.float32)
+    all_sems = pltpu.SemaphoreType.DMA((2, HEADS))
+    few_sems = pltpu.SemaphoreType.DMA((2, each))
+    vmem = pl.BlockSpec(memory_space=pltpu.VMEM)
+    out_q, out_k, out_v, out_rq = pl.pallas_call(
+        functools.partial(kernel, factor),
+        out_shape=(
+            jax.ShapeDtypeStruct((rows, width), jnp.bfloat16),
+            jax.ShapeDtypeStruct((rows, width), jnp.bfloat16),
+            jax.ShapeDtypeStruct((rows, width), jnp.bfloat16),
+            jax.ShapeDtypeStruct((regs, width), jnp.bfloat16),
+        ),
+        in_specs=[pl.BlockSpec(memory_space=pl.ANY)] * 6 + [vmem],
+        out_specs=(vmem,) * 4,
+        scratch_shapes=[
+            pltpu.VMEM((rows + regs, width), jnp.bfloat16),
+            pltpu.VMEM((rows + regs, width), jnp.bfloat16),
+            pltpu.VMEM((rows, width), jnp.bfloat16),
+            pltpu.VMEM((rows, width), jnp.bfloat16),
+            all_states, all_states,
+            few_states, few_states, few_states, few_states, few_states,
+            all_states,
+            pltpu.VMEM((2, HEADS, HEAD, HEAD), jnp.bfloat16),
+            pltpu.VMEM((rows + regs, width), jnp.float32),
+            pltpu.VMEM((rows, width), jnp.float32),
+            pltpu.VMEM((rows, width), jnp.float32),
+            pltpu.SemaphoreType.DMA((6,)),
+            all_sems, all_sems,
+            few_sems, few_sems, few_sems, few_sems,
+            few_sems, few_sems, few_sems, all_sems,
+        ],
+        compiler_params=pltpu.CompilerParams(
+            collective_id=0, has_side_effects=True, vmem_limit_bytes=40 * 1024 * 1024
+        ),
+    )(
+        query_rows, key_rows, value_rows, out_grad, reg_query, reg_out_grad,
+        reg_offset.reshape(1, regs),
+    )
+    return out_q, out_k, out_v, out_rq
+
+
 def solution(mesh):
     placed = (
         P(("grp", "ctx", "sub"), None),
@@ -130,7 +423,7 @@
         P(("grp", "ctx", "sub")),
     )
     return jax.shard_map(
-        local,
+        fused if mesh.shape["sub"] == 4 else local,
         mesh=mesh,
         in_specs=placed,
         out_specs=(

time: 113 us -> 38.2 us (0.34)
  blocking collectives: 47.6 us -> 0 us
  Pallas kernels: 0 us -> 27.1 us
  matrix products: 19.5 us -> 0 us
  between operations: 14.3 us -> 0.66 us
  waiting for transfers between devices: 12.1 us -> 0 us
  other arithmetic: 10.1 us -> 0 us
  local copies, waits for them, and re-layouts: 8.25 us -> 9.95 us
    all_gather x4 -> x0, blocking collectives: 47.6 us -> none  [the longest x2 33.6 us: carried_in(): pieces = lax.all_gather(value, axis)]
    pallas_call x0 -> x1, Pallas kernels: none -> 27.1 us  [fused(): pl.pallas_call(functools.partial(kernel, factor), out_shape=(jax.ShapeDty...]
    dot_general x15 -> x0, matrix products: 19.5 us -> none  [the longest x1 2.54 us: local(): jnp.einsum('hjs,jhe->she', reg_qk_scores, regg_heads, preferred_element_t...]
    all_gather x2 -> x0, waiting for transfers between devices: 12.1 us -> none  [the longest x1 12.1 us: local(): lax.all_gather(grad_local[None], 'sub', axis=0, tiled=True)]
    reduce_sum x2 -> x0, other arithmetic: 5.63 us -> none  [the longest x1 2.82 us: local(): inner_kv = jnp.sum(jnp.where(earlier_mask, every_kv, zero_value), axis=0)]
    unnamed x37 -> x18, local copies, waits for them, and re-layouts: 4.97 us -> 9.95 us
    select_n x6 -> x0, other arithmetic: 3.07 us -> none  [hop(): return jnp.where(position < mine, longer, running)]
    reshape x2 -> x0, local copies, waits for them, and re-layouts: 2.18 us -> none  [the longest x1 1.33 us: local(): grad_heads = out_grad.reshape(row_count, HEADS, HEAD)]
  transfers between devices with their start and end apart: 2 -> 0, of which waited for: 1 -> 0; matrix products, arithmetic and copies ran while one was open for 14% -> 0% of each run, Pallas kernels for 0% -> 0%
where the time goes in v1:
time: 38.2 us; the launch traced here: 37.8 us
  Pallas kernels  27.1 us (71%)
  local copies, waits for them, and re-layouts  9.95 us (26%)
  between operations  0.66 us (2%)
    pallas_call x1, Pallas kernels, fused(): pl.pallas_call(functools.partial(kernel, factor), out_shape=(jax.ShapeDty...  27.1 us
    unnamed x18, local copies, waits for them, and re-layouts  9.95 us

profile of v1, /device:TPU:0, one launch (start us, length us, event | category | flops | bytes accessed | tf_op | source)
XLA Modules:
  0.0 37.8 jit_solution(11451673441492298044)
XLA Ops:
  0.6 0.0 copy-start.6
  0.6 0.7 %copy-done.6 = s32[192]{0:T(256)S(1)} copy-done((s32[192]{0:T(256)S(1)}, s32[192]{0:T(256)}, u32[]{:S(2)}) %copy-start.6) | copy-done | bytes 792
  1.3 0.0 copy-start
  1.3 1.0 %copy-done = bf16[256,1024]{1,0:T(8,128)(2,1)S(1)} copy-done((bf16[256,1024]{1,0:T(8,128)(2,1)S(1)}, bf16[256,1024]{1,0:T(8,128)(2,1)}, u32[]{:S(2)}) %copy-start) | copy-done | bytes 524312
  2.4 0.0 copy-start.1
  2.4 1.0 %copy-done.1 = bf16[256,1024]{1,0:T(8,128)(2,1)S(1)} copy-done((bf16[256,1024]{1,0:T(8,128)(2,1)S(1)}, bf16[256,1024]{1,0:T(8,128)(2,1)}, u32[]{:S(2)}) %copy-start.1) | copy-done | bytes 524312
  3.4 0.0 copy-start.2
  3.4 1.0 %copy-done.2 = bf16[256,1024]{1,0:T(8,128)(2,1)S(1)} copy-done((bf16[256,1024]{1,0:T(8,128)(2,1)S(1)}, bf16[256,1024]{1,0:T(8,128)(2,1)}, u32[]{:S(2)}) %copy-start.2) | copy-done | bytes 524312
  4.4 0.0 copy-start.3
  4.4 1.0 %copy-done.3 = bf16[256,1024]{1,0:T(8,128)(2,1)S(1)} copy-done((bf16[256,1024]{1,0:T(8,128)(2,1)S(1)}, bf16[256,1024]{1,0:T(8,128)(2,1)}, u32[]{:S(2)}) %copy-start.3) | copy-done | bytes 524312
  5.5 0.0 copy-start.4
  5.5 1.0 %copy-done.4 = bf16[192,1024]{1,0:T(8,128)(2,1)S(1)} copy-done((bf16[192,1024]{1,0:T(8,128)(2,1)S(1)}, bf16[192,1024]{1,0:T(8,128)(2,1)}, u32[]{:S(2)}) %copy-start.4) | copy-done | bytes 393240
  6.5 0.0 copy-start.5
  6.5 1.0 %copy-done.5 = bf16[192,1024]{1,0:T(8,128)(2,1)S(1)} copy-done((bf16[192,1024]{1,0:T(8,128)(2,1)S(1)}, bf16[192,1024]{1,0:T(8,128)(2,1)}, u32[]{:S(2)}) %copy-start.5) | copy-done | bytes 393240
  7.5 27.1 %shard_map.102 = (bf16[256,1024]{1,0:T(8,128)(2,1)S(1)}, bf16[256,1024]{1,0:T(8,128)(2,1)S(1)}, bf16[256,1024]{1,0:T(8,128)(2,1)S(1)}, bf16[192,1024]{1,0:T(8,128)(2,1)S(1)}) custom-call(bf16[256,1024]{1,0:T(8,128)(2,1)S(1)} %copy-done, bf16[256,1024]{1,0:T(8,128)(2,1)S(1)} %copy-done.1, bf16[256,1024]{1,0:T(8,128)(2,1)S(1)} %copy-done.2, ...), custom_call_target="tpu_custom_call" | custom-call | tf_op jit(solution)/shard_map/pallas_call | solution.py:378
  34.6 0.8 %copy.15 = bf16[256,1024]{1,0:T(8,128)(2,1)} copy(bf16[256,1024]{1,0:T(8,128)(2,1)S(1)} %get-tuple-element.8) | data formatting | bytes 1048576
  35.4 0.8 %copy.16 = bf16[256,1024]{1,0:T(8,128)(2,1)} copy(bf16[256,1024]{1,0:T(8,128)(2,1)S(1)} %get-tuple-element.9) | data formatting | bytes 1048576
  36.2 0.8 %copy.17 = bf16[256,1024]{1,0:T(8,128)(2,1)} copy(bf16[256,1024]{1,0:T(8,128)(2,1)S(1)} %get-tuple-element.10) | data formatting | bytes 1048576
  37.0 0.7 %copy.18 = bf16[192,1024]{1,0:T(8,128)(2,1)} copy(bf16[192,1024]{1,0:T(8,128)(2,1)S(1)} %get-tuple-element.11) | data formatting | bytes 786432
Async XLA Ops:
  0.6 0.7 %copy-start.6 = (s32[192]{0:T(256)S(1)}, s32[192]{0:T(256)}, u32[]{:S(2)}) copy-start(s32[192]{0:T(256)} %param.13) | copy-start | bytes 2308
  1.3 1.0 %copy-start = (bf16[256,1024]{1,0:T(8,128)(2,1)S(1)}, bf16[256,1024]{1,0:T(8,128)(2,1)}, u32[]{:S(2)}) copy-start(bf16[256,1024]{1,0:T(8,128)(2,1)} %q_hbm.1) | copy-start | bytes 1572868
  2.4 1.0 %copy-start.1 = (bf16[256,1024]{1,0:T(8,128)(2,1)S(1)}, bf16[256,1024]{1,0:T(8,128)(2,1)}, u32[]{:S(2)}) copy-start(bf16[256,1024]{1,0:T(8,128)(2,1)} %k_hbm.1) | copy-start | bytes 1572868
  3.4 1.0 %copy-start.2 = (bf16[256,1024]{1,0:T(8,128)(2,1)S(1)}, bf16[256,1024]{1,0:T(8,128)(2,1)}, u32[]{:S(2)}) copy-start(bf16[256,1024]{1,0:T(8,128)(2,1)} %v_hbm.1) | copy-start | bytes 1572868
  4.4 1.0 %copy-start.3 = (bf16[256,1024]{1,0:T(8,128)(2,1)S(1)}, bf16[256,1024]{1,0:T(8,128)(2,1)}, u32[]{:S(2)}) copy-start(bf16[256,1024]{1,0:T(8,128)(2,1)} %g_hbm.1) | copy-start | bytes 1572868
  5.5 1.0 %copy-start.4 = (bf16[192,1024]{1,0:T(8,128)(2,1)S(1)}, bf16[192,1024]{1,0:T(8,128)(2,1)}, u32[]{:S(2)}) copy-start(bf16[192,1024]{1,0:T(8,128)(2,1)} %rq_hbm.1) | copy-start | bytes 1179652
  6.5 1.0 %copy-start.5 = (bf16[192,1024]{1,0:T(8,128)(2,1)S(1)}, bf16[192,1024]{1,0:T(8,128)(2,1)}, u32[]{:S(2)}) copy-start(bf16[192,1024]{1,0:T(8,128)(2,1)} %rg_hbm.1) | copy-start | bytes 1179652

commit v2 on v1

--- a/solution.py
+++ b/solution.py
@@ -364,6 +364,19 @@
             pair_copy(c, (2 * side + c) * each + i).wait_send()
 
 
+def store_all(*refs):
+    sources, results, held, in_sem, out_sem = refs[:4], refs[4:8], refs[8:12], refs[12], refs[13]
+    loads = [pltpu.make_async_copy(sources[i], held[i], in_sem.at[i]) for i in range(4)]
+    stores = [pltpu.make_async_copy(held[i], results[i], out_sem.at[i]) for i in range(4)]
+    for load in loads:
+        load.start()
+    for load, store in zip(loads, stores):
+        load.wait()
+        store.start()
+    for store in stores:
+        store.wait()
+
+
 def fused(query_rows, key_rows, value_rows, out_grad, reg_query, reg_out_grad, reg_offset):
     rows, width = query_rows.shape
     regs = reg_query.shape[0]
@@ -375,15 +388,17 @@
     all_sems = pltpu.SemaphoreType.DMA((2, HEADS))
     few_sems = pltpu.SemaphoreType.DMA((2, each))
     vmem = pl.BlockSpec(memory_space=pltpu.VMEM)
-    out_q, out_k, out_v, out_rq = pl.pallas_call(
+    hbm = pl.BlockSpec(memory_space=pltpu.HBM)
+    shapes = (
+        jax.ShapeDtypeStruct((rows, width), jnp.bfloat16),
+        jax.ShapeDtypeStruct((rows, width), jnp.bfloat16),
+        jax.ShapeDtypeStruct((rows, width), jnp.bfloat16),
+        jax.ShapeDtypeStruct((regs, width), jnp.bfloat16),
+    )
+    results = pl.pallas_call(
         functools.partial(kernel, factor),
-        out_shape=(
-            jax.ShapeDtypeStruct((rows, width), jnp.bfloat16),
-            jax.ShapeDtypeStruct((rows, width), jnp.bfloat16),
-            jax.ShapeDtypeStruct((rows, width), jnp.bfloat16),
-            jax.ShapeDtypeStruct((regs, width), jnp.bfloat16),
-        ),
-        in_specs=[pl.BlockSpec(memory_space=pl.ANY)] * 6 + [vmem],
+        out_shape=shapes,
+        in_specs=[hbm] * 6 + [vmem],
         out_specs=(vmem,) * 4,
         scratch_shapes=[
             pltpu.VMEM((rows + regs, width), jnp.bfloat16),
@@ -403,13 +418,21 @@
             few_sems, few_sems, few_sems, all_sems,
         ],
         compiler_params=pltpu.CompilerParams(
-            collective_id=0, has_side_effects=True, vmem_limit_bytes=40 * 1024 * 1024
+            collective_id=0, has_side_effects=True, vmem_limit_bytes=63400 * 1024
         ),
     )(
         query_rows, key_rows, value_rows, out_grad, reg_query, reg_out_grad,
         reg_offset.reshape(1, regs),
     )
-    return out_q, out_k, out_v, out_rq
+    return pl.pallas_call(
+        store_all,
+        out_shape=shapes,
+        in_specs=[hbm] * 4,
+        out_specs=(hbm,) * 4,
+        scratch_shapes=[pltpu.VMEM(shape.shape, shape.dtype) for shape in shapes]
+        + [pltpu.SemaphoreType.DMA((4,)), pltpu.SemaphoreType.DMA((4,))],
+        compiler_params=pltpu.CompilerParams(vmem_limit_bytes=63400 * 1024),
+    )(*results)
 
 
 def solution(mesh):

time: 38.2 us -> 32.3 us (0.85)
  local copies, waits for them, and re-layouts: 9.95 us -> 0 us
  Pallas kernels: 27.1 us -> 31.5 us
    unnamed x18 -> x0, local copies, waits for them, and re-layouts: 9.95 us -> none
    pallas_call x1 -> x2, Pallas kernels: 27.1 us -> 31.5 us  [the longest x1 29.1 us: fused(): pl.pallas_call(functools.partial(kernel, factor), out_shape=shapes, in_sp...]
where the time goes in v2:
time: 32.3 us; the launch traced here: 32.1 us
  Pallas kernels  31.5 us (98%)
  between operations  0.64 us (2%)
    pallas_call x1, Pallas kernels, fused(): pl.pallas_call(functools.partial(kernel, factor), out_shape=shapes, in_sp...  29.1 us
    pallas_call x1, Pallas kernels, fused(): pl.pallas_call(store_all, out_shape=shapes, in_specs=[hbm] * 4, out_specs...  2.37 us

profile of v2, /device:TPU:0, one launch (start us, length us, event | category | flops | bytes accessed | tf_op | source)
XLA Modules:
  0.0 32.1 jit_solution(13170912727269248237)
XLA Ops:
  0.6 29.1 %shard_map.102 = (bf16[256,1024]{1,0:T(8,128)(2,1)}, bf16[256,1024]{1,0:T(8,128)(2,1)}, bf16[256,1024]{1,0:T(8,128)(2,1)}, bf16[192,1024]{1,0:T(8,128)(2,1)}) custom-call(bf16[256,1024]{1,0:T(8,128)(2,1)} %q_hbm.1, bf16[256,1024]{1,0:T(8,128)(2,1)} %k_hbm.1, bf16[256,1024]{1,0:T(8,128)(2,1)} %v_hbm.1, bf16[256,1024]{1,0:T(8,128)(2,1)} %g_hbm.1, ...), custom_call_target="tpu_custom_call" | custom-call | tf_op jit(solution)/shard_map/pallas_call | solution.py:398
  29.8 2.4 %shard_map.103 = (bf16[256,1024]{1,0:T(8,128)(2,1)}, bf16[256,1024]{1,0:T(8,128)(2,1)}, bf16[256,1024]{1,0:T(8,128)(2,1)}, bf16[192,1024]{1,0:T(8,128)(2,1)}) custom-call(bf16[256,1024]{1,0:T(8,128)(2,1)} %get-tuple-element.8.refs_0_, bf16[256,1024]{1,0:T(8,128)(2,1)} %get-tuple-element.9.refs_1_, bf16[256,1024]{1,0:T(8,128)(2,1)} %get-tuple-element.10.refs_2_, ...), custom_call_target="tpu_custom_call" | custom-call | tf_op jit(solution)/shard_map/pallas_call | solution.py:427

commit v3 on v2

--- a/solution.py
+++ b/solution.py
@@ -11,6 +11,7 @@
 HEADS = 8
 HEAD = 128
 MESH = pl.DeviceIdType.MESH
+PARTS = 2
 
 
 def carried_in(value, axis, join, neutral, backward):
@@ -140,6 +141,7 @@
 ):
     ctx_count, sub_count = lax.axis_size("ctx"), lax.axis_size("sub")
     each = HEADS // sub_count
+    units = each * PARTS
     z, s = lax.axis_index("ctx"), lax.axis_index("sub")
     a, c = s // 2, s % 2
     partner = {"sub": 2 * a + 1 - c}
@@ -173,6 +175,9 @@
     def cols(h):
         return pl.ds(pl.multiple_of(h * HEAD, HEAD), HEAD)
 
+    def whole(h):
+        return pl.ds(h * PARTS, PARTS)
+
     def remote(src, dst, send, recv, target):
         return pltpu.make_async_remote_copy(
             src_ref=src, dst_ref=dst, send_sem=send, recv_sem=recv,
@@ -180,7 +185,7 @@
         )
 
     def pair_copy(k, h):
-        return remote(mine.at[k, h], pair.at[k, h], pair_send.at[k, h], pair_recv.at[k, h], partner)
+        return remote(mine.at[k, whole(h)], pair.at[k, whole(h)], pair_send.at[k, h], pair_recv.at[k, h], partner)
 
     def cross_copy(k, i):
         return remote(
@@ -194,25 +199,26 @@
         )
 
     def own_copy(k, i):
-        h = s * each + i
+        h = s * units + i
         return remote(full.at[k, h], full.at[k, h], own_send.at[k, i], full_recv.at[k, h], partner)
 
     def other_copy(k, i):
         return remote(
-            other.at[k, i], full.at[k, s * each + i], other_send.at[k, i],
-            full_recv.at[k, s * each + i], across,
+            other.at[k, i], full.at[k, s * units + i], other_send.at[k, i],
+            full_recv.at[k, s * units + i], across,
         )
 
     def relay_copy(k, i):
-        h = across["sub"] * each + i
+        h = across["sub"] * units + i
         return remote(full.at[k, h], full.at[k, h], relay_send.at[k, i], full_recv.at[k, h], partner)
 
     first = jnp.where(2 * z >= ctx_count, 1, 0)
     kinds = (first, 1 - first)
 
     def state(h):
-        mine[0, h] = contract(ka[:, cols(h)], va[:, cols(h)], 0, 0)
-        mine[1, h] = contract(qa[:, cols(h)], ga[:, cols(h)], 0, 0)
+        piece = (PARTS, HEAD // PARTS, HEAD)
+        mine[0, whole(h)] = contract(ka[:, cols(h)], va[:, cols(h)], 0, 0).reshape(piece)
+        mine[1, whole(h)] = contract(qa[:, cols(h)], ga[:, cols(h)], 0, 0).reshape(piece)
 
     for load in loads:
         load.wait()
@@ -226,20 +232,18 @@
             pair_copy(k, (2 * (1 - a) + 1 - c) * each + i).start()
     for i in range(each):
         state(across["sub"] * each + i)
+    for k in kinds:
+        for i in range(each):
+            h = across["sub"] * each + i
+            pair_copy(k, h).wait_recv()
+            cross_out[k, whole(i)] = mine[k, whole(h)] + pair[k, whole(h)]
+            for part in range(PARTS):
+                cross_copy(k, i * PARTS + part).start()
     for i in range(each):
         state((2 * a + 1 - c) * each + i)
     for i in range(each):
         for k in kinds:
             pair_copy(k, (2 * a + 1 - c) * each + i).start()
-
-    for k in kinds:
-        for i in range(each):
-            h = across["sub"] * each + i
-            pair_copy(k, h).wait_recv()
-            cross_out[k, i] = mine[k, h] + pair[k, h]
-    for k in kinds:
-        for i in range(each):
-            cross_copy(k, i).start()
     for i in range(each):
         state(s * each + i)
     for side in range(2):
@@ -274,8 +278,9 @@
         target = jnp.where(k == 0, z + 1, z - 1)
         ahead = a == k
         for i in range(each):
-            h = s * each + i
-            pair_copy(k, h).wait_recv()
+            pair_copy(k, s * each + i).wait_recv()
+        for i in range(units):
+            h = s * units + i
             cross_copy(k, i).wait_recv()
 
             @pl.when(has_in)
@@ -284,7 +289,7 @@
 
             @pl.when(jnp.logical_not(has_in))
             def _():
-                chain_in[k, i] = jnp.zeros((HEAD, HEAD), jnp.float32)
+                chain_in[k, i] = jnp.zeros((HEAD // PARTS, HEAD), jnp.float32)
 
             @pl.when(has_out)
             def _():
@@ -299,58 +304,63 @@
             full[k, h] = carried + jnp.where(ahead, zero, cross_in[k, i])
             own_copy(k, i).start()
 
+    def relay(k):
+        for i in range(units):
+            h = across["sub"] * units + i
+            remote(
+                other.at[k, i], full.at[k, h], other_send.at[k, i], full_recv.at[k, h], across
+            ).wait_recv()
+            relay_copy(k, i).start()
+
+    def full_wait(h):
+        for k in range(2):
+            for part in range(PARTS):
+                u = h * PARTS + part
+                remote(
+                    full.at[k, u], full.at[k, u], own_send.at[0, 0], full_recv.at[k, u], partner
+                ).wait_recv()
+
+    def finish(h):
+        at = cols(h)
+        square = (HEAD, HEAD)
+        joined = full[1 - c, whole(h)] + pair[1 - c, whole(h)]
+        full16[1 - c, h] = joined.reshape(square).astype(jnp.bfloat16)
+        full16[c, h] = full[c, whole(h)].reshape(square).astype(jnp.bfloat16)
+        before, after = full16[0, h], full16[1, h]
+        sums = (acc_q[:, at] + contract(ga[:, at], before, 1, 1)) * factor
+        out_q[:, at] = sums[:rows].astype(jnp.bfloat16)
+        out_rq[:, at] = sums[rows:].astype(jnp.bfloat16)
+        out_k[:, at] = ((acc_k[:, at] + contract(va[:, at], after, 1, 1)) * factor).astype(jnp.bfloat16)
+        out_v[:, at] = ((acc_v[:, at] + contract(ka[:, at], after, 1, 0)) * factor).astype(jnp.bfloat16)
+
     some_scores(0, 3)
     chain(kinds[0])
-    some_scores(3, 6)
+    some_scores(3, 5)
     chain(kinds[1])
-    some_scores(6, HEADS)
-
-    for k in kinds:
-        for i in range(each):
-            other_copy_in = remote(
-                other.at[k, i], full.at[k, across["sub"] * each + i], other_send.at[k, i],
-                full_recv.at[k, across["sub"] * each + i], across,
-            )
-            other_copy_in.wait_recv()
-            relay_copy(k, i).start()
-
-    def full_wait(k, h):
-        remote(full.at[k, h], full.at[k, h], own_send.at[0, 0], full_recv.at[k, h], partner).wait_recv()
-
+    relay(kinds[0])
+    some_scores(5, HEADS)
     for side in range(2):
         for i in range(each):
             pair_copy(1 - c, (2 * side + 1 - c) * each + i).wait_recv()
-
-    def finish(h):
-        at = cols(h)
-        full16[1 - c, h] = (full[1 - c, h] + pair[1 - c, h]).astype(jnp.bfloat16)
-        full16[c, h] = full[c, h].astype(jnp.bfloat16)
-        before, after = full16[0, h], full16[1, h]
-        whole = (acc_q[:, at] + contract(ga[:, at], before, 1, 1)) * factor
-        out_q[:, at] = whole[:rows].astype(jnp.bfloat16)
-        out_rq[:, at] = whole[rows:].astype(jnp.bfloat16)
-        out_k[:, at] = ((acc_k[:, at] + contract(va[:, at], after, 1, 1)) * factor).astype(jnp.bfloat16)
-        out_v[:, at] = ((acc_v[:, at] + contract(ka[:, at], after, 1, 0)) * factor).astype(jnp.bfloat16)
-
     for i in range(each):
         finish(s * each + i)
     for i in range(each):
+        h = (2 * a + 1 - c) * each + i
+        full_wait(h)
+        finish(h)
+    relay(kinds[1])
+    for i in range(each):
         finish(across["sub"] * each + i)
     for i in range(each):
-        h = (2 * a + 1 - c) * each + i
-        full_wait(0, h)
-        full_wait(1, h)
-        finish(h)
-    for i in range(each):
         h = (2 * (1 - a) + 1 - c) * each + i
-        full_wait(0, h)
-        full_wait(1, h)
+        full_wait(h)
         finish(h)
 
     for k in range(2):
         for i in range(each):
             for side in range(2):
                 pair_copy(k, (2 * side + 1 - c) * each + i).wait_send()
+        for i in range(units):
             cross_copy(k, i).wait_send()
             other_copy(k, i).wait_send()
             own_copy(k, i).wait_send()
@@ -383,10 +393,11 @@
     sub_count = lax.axis_size("sub")
     factor = 1.0 / math.sqrt(HEAD * rows * lax.axis_size("ctx") * sub_count)
     each = HEADS // sub_count
-    all_states = pltpu.VMEM((2, HEADS, HEAD, HEAD), jnp.float32)
-    few_states = pltpu.VMEM((2, each, HEAD, HEAD), jnp.float32)
+    all_states = pltpu.VMEM((2, HEADS * PARTS, HEAD // PARTS, HEAD), jnp.float32)
+    few_states = pltpu.VMEM((2, each * PARTS, HEAD // PARTS, HEAD), jnp.float32)
     all_sems = pltpu.SemaphoreType.DMA((2, HEADS))
-    few_sems = pltpu.SemaphoreType.DMA((2, each))
+    unit_sems = pltpu.SemaphoreType.DMA((2, HEADS * PARTS))
+    few_sems = pltpu.SemaphoreType.DMA((2, each * PARTS))
     vmem = pl.BlockSpec(memory_space=pltpu.VMEM)
     hbm = pl.BlockSpec(memory_space=pltpu.HBM)
     shapes = (
@@ -415,7 +426,7 @@
             pltpu.SemaphoreType.DMA((6,)),
             all_sems, all_sems,
             few_sems, few_sems, few_sems, few_sems,
-            few_sems, few_sems, few_sems, all_sems,
+            few_sems, few_sems, few_sems, unit_sems,
         ],
         compiler_params=pltpu.CompilerParams(
             collective_id=0, has_side_effects=True, vmem_limit_bytes=63400 * 1024

time: 32.3 us -> 30.8 us (0.954); the launches traced: 32.1 us -> 30.3 us
  Pallas kernels: 31.5 us -> 29.6 us
    pallas_call x1, Pallas kernels: 29.1 us -> 27.3 us  [fused(): pl.pallas_call(functools.partial(kernel, factor), out_shape=shapes, in_sp...]
where the time goes in v3:
time: 30.8 us; the launch traced here: 30.3 us
  Pallas kernels  29.6 us (96%)
  between operations  0.64 us (2%)
    pallas_call x1, Pallas kernels, fused(): pl.pallas_call(functools.partial(kernel, factor), out_shape=shapes, in_sp...  27.3 us
    pallas_call x1, Pallas kernels, fused(): pl.pallas_call(store_all, out_shape=shapes, in_specs=[hbm] * 4, out_specs...  2.37 us

profile of v3, /device:TPU:0, one launch (start us, length us, event | category | flops | bytes accessed | tf_op | source)
XLA Modules:
  0.0 30.3 jit_solution(10363439255738455055)
XLA Ops:
  0.6 27.3 %shard_map.102 = (bf16[256,1024]{1,0:T(8,128)(2,1)}, bf16[256,1024]{1,0:T(8,128)(2,1)}, bf16[256,1024]{1,0:T(8,128)(2,1)}, bf16[192,1024]{1,0:T(8,128)(2,1)}) custom-call(bf16[256,1024]{1,0:T(8,128)(2,1)} %q_hbm.1, bf16[256,1024]{1,0:T(8,128)(2,1)} %k_hbm.1, bf16[256,1024]{1,0:T(8,128)(2,1)} %v_hbm.1, bf16[256,1024]{1,0:T(8,128)(2,1)} %g_hbm.1, ...), custom_call_target="tpu_custom_call" | custom-call | tf_op jit(solution)/shard_map/pallas_call | solution.py:409
  27.9 2.4 %shard_map.103 = (bf16[256,1024]{1,0:T(8,128)(2,1)}, bf16[256,1024]{1,0:T(8,128)(2,1)}, bf16[256,1024]{1,0:T(8,128)(2,1)}, bf16[192,1024]{1,0:T(8,128)(2,1)}) custom-call(bf16[256,1024]{1,0:T(8,128)(2,1)} %get-tuple-element.8.refs_0_, bf16[256,1024]{1,0:T(8,128)(2,1)} %get-tuple-element.9.refs_1_, bf16[256,1024]{1,0:T(8,128)(2,1)} %get-tuple-element.10.refs_2_, ...), custom_call_target="tpu_custom_call" | custom-call | tf_op jit(solution)/shard_map/pallas_call | solution.py:438

commit v4 on v3

--- a/solution.py
+++ b/solution.py
@@ -132,9 +132,9 @@
 
 def kernel(
     factor,
-    q_hbm, k_hbm, v_hbm, g_hbm, rq_hbm, rg_hbm, off_ref,
+    q_hbm, k_hbm, v_hbm, g_hbm, rq_hbm, rg_hbm, off_hbm,
     out_q, out_k, out_v, out_rq,
-    qa, ga, ka, va, mine, pair, cross_out, cross_in, chain_in, chain_out, other, full, full16,
+    off_ref, qa, ga, ka, va, mine, pair, cross_out, cross_in, chain_in, chain_out, other, full, full16,
     acc_q, acc_k, acc_v,
     load_sem, pair_send, pair_recv, cross_send, cross_recv, chain_send, chain_recv,
     own_send, other_send, relay_send, full_recv,
@@ -156,8 +156,10 @@
         pltpu.make_async_copy(rq_hbm, qa.at[pl.ds(rows, regs)], load_sem.at[4]),
         pltpu.make_async_copy(rg_hbm, ga.at[pl.ds(rows, regs)], load_sem.at[5]),
     ]
+    load_offset = pltpu.make_async_copy(off_hbm, off_ref, load_sem.at[6])
     for load in loads:
         load.start()
+    load_offset.start()
 
     barrier = pltpu.get_barrier_semaphore()
     has_prev, has_next = z > 0, z < ctx_count - 1
@@ -333,6 +335,7 @@
         out_k[:, at] = ((acc_k[:, at] + contract(va[:, at], after, 1, 1)) * factor).astype(jnp.bfloat16)
         out_v[:, at] = ((acc_v[:, at] + contract(ka[:, at], after, 1, 0)) * factor).astype(jnp.bfloat16)
 
+    load_offset.wait()
     some_scores(0, 3)
     chain(kinds[0])
     some_scores(3, 5)
@@ -375,16 +378,11 @@
 
 
 def store_all(*refs):
-    sources, results, held, in_sem, out_sem = refs[:4], refs[4:8], refs[8:12], refs[12], refs[13]
-    loads = [pltpu.make_async_copy(sources[i], held[i], in_sem.at[i]) for i in range(4)]
-    stores = [pltpu.make_async_copy(held[i], results[i], out_sem.at[i]) for i in range(4)]
-    for load in loads:
-        load.start()
-    for load, store in zip(loads, stores):
-        load.wait()
-        store.start()
-    for store in stores:
-        store.wait()
+    copies = [pltpu.make_async_copy(refs[i], refs[4 + i], refs[8].at[i]) for i in range(4)]
+    for copy in copies:
+        copy.start()
+    for copy in copies:
+        copy.wait()
 
 
 def fused(query_rows, key_rows, value_rows, out_grad, reg_query, reg_out_grad, reg_offset):
@@ -409,9 +407,10 @@
     results = pl.pallas_call(
         functools.partial(kernel, factor),
         out_shape=shapes,
-        in_specs=[hbm] * 6 + [vmem],
+        in_specs=[hbm] * 7,
         out_specs=(vmem,) * 4,
         scratch_shapes=[
+            pltpu.VMEM((1, regs), jnp.int32),
             pltpu.VMEM((rows + regs, width), jnp.bfloat16),
             pltpu.VMEM((rows + regs, width), jnp.bfloat16),
             pltpu.VMEM((rows, width), jnp.bfloat16),
@@ -423,26 +422,28 @@
             pltpu.VMEM((rows + regs, width), jnp.float32),
             pltpu.VMEM((rows, width), jnp.float32),
             pltpu.VMEM((rows, width), jnp.float32),
-            pltpu.SemaphoreType.DMA((6,)),
+            pltpu.SemaphoreType.DMA((7,)),
             all_sems, all_sems,
             few_sems, few_sems, few_sems, few_sems,
             few_sems, few_sems, few_sems, unit_sems,
         ],
         compiler_params=pltpu.CompilerParams(
-            collective_id=0, has_side_effects=True, vmem_limit_bytes=63400 * 1024
+            collective_id=0, has_side_effects=True, vmem_limit_bytes=40960 * 1024
         ),
     )(
-        query_rows, key_rows, value_rows, out_grad, reg_query, reg_out_grad,
-        reg_offset.reshape(1, regs),
+        *[
+            pltpu.with_memory_space_constraint(array, pltpu.HBM)
+            for array in (query_rows, key_rows, value_rows, out_grad, reg_query, reg_out_grad)
+        ],
+        pltpu.with_memory_space_constraint(reg_offset.reshape(1, regs), pltpu.HBM),
     )
     return pl.pallas_call(
         store_all,
         out_shape=shapes,
-        in_specs=[hbm] * 4,
+        in_specs=[vmem] * 4,
         out_specs=(hbm,) * 4,
-        scratch_shapes=[pltpu.VMEM(shape.shape, shape.dtype) for shape in shapes]
-        + [pltpu.SemaphoreType.DMA((4,)), pltpu.SemaphoreType.DMA((4,))],
-        compiler_params=pltpu.CompilerParams(vmem_limit_bytes=63400 * 1024),
+        scratch_shapes=[pltpu.SemaphoreType.DMA((4,))],
+        compiler_params=pltpu.CompilerParams(vmem_limit_bytes=1024 * 1024),
     )(*results)
 
 

time: 30.8 us -> 27.7 us (0.90)
  Pallas kernels: 29.6 us -> 26.6 us
    pallas_call x1, Pallas kernels: 27.3 us -> 25.3 us  [fused(): pl.pallas_call(functools.partial(kernel, factor), out_shape=shapes, in_sp...]
    pallas_call x1, Pallas kernels: 2.37 us -> 1.3 us  [fused(): pl.pallas_call(store_all, out_shape=shapes, in_specs=[vmem] * 4, out_spec...]
where the time goes in v4:
time: 27.7 us; the launch traced here: 27.3 us
  Pallas kernels  26.6 us (96%)
  between operations  0.64 us (2%)
    pallas_call x1, Pallas kernels, fused(): pl.pallas_call(functools.partial(kernel, factor), out_shape=shapes, in_sp...  25.3 us
    pallas_call x1, Pallas kernels, fused(): pl.pallas_call(store_all, out_shape=shapes, in_specs=[vmem] * 4, out_spec...  1.3 us

profile of v4, /device:TPU:0, one launch (start us, length us, event | category | flops | bytes accessed | tf_op | source)
XLA Modules:
  0.0 27.3 jit_solution(7960238285274096222)
XLA Ops:
  0.6 25.3 %shard_map.102 = (bf16[256,1024]{1,0:T(8,128)(2,1)S(1)}, bf16[256,1024]{1,0:T(8,128)(2,1)S(1)}, bf16[256,1024]{1,0:T(8,128)(2,1)S(1)}, bf16[192,1024]{1,0:T(8,128)(2,1)S(1)}) custom-call(bf16[256,1024]{1,0:T(8,128)(2,1)} %q_hbm.1, bf16[256,1024]{1,0:T(8,128)(2,1)} %k_hbm.1, bf16[256,1024]{1,0:T(8,128)(2,1)} %v_hbm.1, bf16[256,1024]{1,0:T(8,128)(2,1)} %g_hbm.1, ...), custom_call_target="tpu_custom_call" | custom-call | tf_op jit(solution)/shard_map/pallas_call | solution.py:407
  26.0 1.3 %shard_map.103 = (bf16[256,1024]{1,0:T(8,128)(2,1)}, bf16[256,1024]{1,0:T(8,128)(2,1)}, bf16[256,1024]{1,0:T(8,128)(2,1)}, bf16[192,1024]{1,0:T(8,128)(2,1)}) custom-call(bf16[256,1024]{1,0:T(8,128)(2,1)S(1)} %get-tuple-element.8.refs_0_, bf16[256,1024]{1,0:T(8,128)(2,1)S(1)} %get-tuple-element.9.refs_1_, bf16[256,1024]{1,0:T(8,128)(2,1)S(1)} %get-tuple-element.10.refs_2_, ...), custom_call_target="tpu_custom_call" | custom-call | tf_op jit(solution)/shard_map/pallas_call | solution.py:440

commit v5 on v4

--- a/solution.py
+++ b/solution.py
@@ -336,12 +336,12 @@
         out_v[:, at] = ((acc_v[:, at] + contract(ka[:, at], after, 1, 0)) * factor).astype(jnp.bfloat16)
 
     load_offset.wait()
-    some_scores(0, 3)
+    some_scores(0, 2)
     chain(kinds[0])
-    some_scores(3, 5)
+    some_scores(2, 4)
     chain(kinds[1])
     relay(kinds[0])
-    some_scores(5, HEADS)
+    some_scores(4, HEADS)
     for side in range(2):
         for i in range(each):
             pair_copy(1 - c, (2 * side + 1 - c) * each + i).wait_recv()

time: 27.7 us -> 28.2 us (1.018)
  Pallas kernels: 26.6 us -> 27.1 us
    pallas_call x1, Pallas kernels: 25.3 us -> 25.8 us  [fused(): pl.pallas_call(functools.partial(kernel, factor), out_shape=shapes, in_sp...]
where the time goes in v5:
time: 28.2 us; the launch traced here: 27.7 us
  Pallas kernels  27.1 us (96%)
  between operations  0.64 us (2%)
    pallas_call x1, Pallas kernels, fused(): pl.pallas_call(functools.partial(kernel, factor), out_shape=shapes, in_sp...  25.8 us
    pallas_call x1, Pallas kernels, fused(): pl.pallas_call(store_all, out_shape=shapes, in_specs=[vmem] * 4, out_spec...  1.3 us

profile of v5, /device:TPU:0, one launch (start us, length us, event | category | flops | bytes accessed | tf_op | source)
XLA Modules:
  0.0 27.7 jit_solution(12820538694926966608)
XLA Ops:
  0.6 25.8 %shard_map.102 = (bf16[256,1024]{1,0:T(8,128)(2,1)S(1)}, bf16[256,1024]{1,0:T(8,128)(2,1)S(1)}, bf16[256,1024]{1,0:T(8,128)(2,1)S(1)}, bf16[192,1024]{1,0:T(8,128)(2,1)S(1)}) custom-call(bf16[256,1024]{1,0:T(8,128)(2,1)} %q_hbm.1, bf16[256,1024]{1,0:T(8,128)(2,1)} %k_hbm.1, bf16[256,1024]{1,0:T(8,128)(2,1)} %v_hbm.1, bf16[256,1024]{1,0:T(8,128)(2,1)} %g_hbm.1, ...), custom_call_target="tpu_custom_call" | custom-call | tf_op jit(solution)/shard_map/pallas_call | solution.py:407
  26.4 1.3 %shard_map.103 = (bf16[256,1024]{1,0:T(8,128)(2,1)}, bf16[256,1024]{1,0:T(8,128)(2,1)}, bf16[256,1024]{1,0:T(8,128)(2,1)}, bf16[192,1024]{1,0:T(8,128)(2,1)}) custom-call(bf16[256,1024]{1,0:T(8,128)(2,1)S(1)} %get-tuple-element.8.refs_0_, bf16[256,1024]{1,0:T(8,128)(2,1)S(1)} %get-tuple-element.9.refs_1_, bf16[256,1024]{1,0:T(8,128)(2,1)S(1)} %get-tuple-element.10.refs_2_, ...), custom_call_target="tpu_custom_call" | custom-call | tf_op jit(solution)/shard_map/pallas_call | solution.py:440
